TPU v7x, 32 devices: a whole 2x2x4 slice. The times are simulated.
32 devices in a mesh: mem: 4 (over z), gx: 4 (over y, core), gy: 2 (over x).
Axes of the slice: x: 2, y: 2, z: 4, core: 2. Of those that a mesh axis runs over, the one named last changes fastest.
Arguments:
- height: float32 [4, 4, 128, 256], P('mem', None, 'gx', 'gy'), may hold values from -4 to 4
- wind: float32 [4, 2, 4, 128, 256], P('mem', None, None, 'gx', 'gy'), may hold values from -0.8 to 0.8
- moisture: float32 [4, 4, 128, 256], P('mem', None, 'gx', 'gy'), may hold values from 0 to 2
- coeffs: float32 [4, 4, 4, 16384], P('mem', None, None, ('gx', 'gy')), may hold values from -6 to 6
- damping: float32 [16384], P(('gx', 'gy')), may hold values from 0.3 to 1
- vmix: float32 [4, 4], replicated, may hold values from -3 to 3
- basis: bfloat16 [16384, 384], P(('gx', 'gy')), may hold values from -0.046875 to 0.046875
- edge_source: int32 [768], replicated, may hold values from 0 to 383
- row_cell: int32 [128], replicated, may hold values from 0 to 15, never falling along the last dimension, each value on 1 to 16 neighbouring positions
- col_cell: int32 [256], replicated, may hold values from 0 to 31, never falling along the last dimension, each value on 1 to 16 neighbouring positions
- cond_rate: float32 [4], replicated, may hold values from 0.05 to 0.5
- saturation: float32 [4], replicated, may hold values from 0.5 to 1.5
- ancestry: int32 [4], replicated, may hold values from 0 to 3
Outputs:
- height_out: float32 [4, 4, 128, 256], P('mem', None, 'gx', 'gy')
- wind_out: float32 [4, 2, 4, 128, 256], P('mem', None, None, 'gx', 'gy')
- moisture_out: float32 [4, 4, 128, 256], P('mem', None, 'gx', 'gy')
- rainfall: float32 [4, 128, 256], P('mem', 'gx', 'gy')
- restricted: float32 [4, 4, 16, 32], P('mem')
- coeffs_out: float32 [4, 4, 4, 16384], P('mem', None, None, ('gx', 'gy'))
Inputs may be any that keep to these rules, and one draw needn't show every extreme that they name: row_cell never falls, and each of the 16 global rows holds 1 to 16 nest rows, one exactly 16. col_cell never falls, and each of the 32 global columns holds 1 to 16 nest columns, one exactly 16.
All inputs are finite; a program needn't handle non-finite values.
Results may differ from a plain program's by a relative error of at most 0.00035.
Values sent between devices are 32-bit elements; how exact they have to be, the bound alone decides.
A program may use at most 64 MiB of HBM per device.

v0:
```python
import jax
import jax.numpy as jnp
from jax import lax
from jax.sharding import PartitionSpec as P

RATIO = 8
ACOUSTIC = 2
acoustic_substep = 0.2
drift_step = 0.4


def extended(block, sides, width):
    for axis, dim in sides:
        count = lax.axis_size(axis)
        forward = [(i, i + 1) for i in range(count - 1)]
        backward = [(target, source) for source, target in forward]
        low = lax.ppermute(
            lax.slice_in_dim(block, block.shape[dim] - width, None, axis=dim), axis, forward
        )
        high = lax.ppermute(lax.slice_in_dim(block, 0, width, axis=dim), axis, backward)
        block = jnp.concatenate([low, block, high], axis=dim)
    return block


def side_values(rim, indices, rim_points, levels):
    table = (indices[None, :] == lax.iota(jnp.int32, rim_points)[:, None]).astype(jnp.float32)
    return jnp.dot(rim, table, precision=lax.Precision.HIGHEST).reshape(4, levels, indices.shape[0])


def frame(padded, sides, flags):
    western_edge, eastern_edge, southern_edge, northern_edge = sides
    at_west, at_east, at_south, at_north = flags
    size_x = padded.shape[2] - 2
    size_y = padded.shape[3] - 2
    current = padded[:, :, 0, 1 : 1 + size_y]
    padded = padded.at[:, :, 0, 1 : 1 + size_y].set(jnp.where(at_west, western_edge, current))
    current = padded[:, :, 1 + size_x, 1 : 1 + size_y]
    padded = padded.at[:, :, 1 + size_x, 1 : 1 + size_y].set(
        jnp.where(at_east, eastern_edge, current)
    )
    current = padded[:, :, 1 : 1 + size_x, 0]
    padded = padded.at[:, :, 1 : 1 + size_x, 0].set(jnp.where(at_south, southern_edge, current))
    current = padded[:, :, 1 : 1 + size_x, 1 + size_y]
    padded = padded.at[:, :, 1 : 1 + size_x, 1 + size_y].set(
        jnp.where(at_north, northern_edge, current)
    )
    return padded


def pick_sides(sides, first, last):
    return tuple((side[first:last] for side in sides))


def body(
    height,
    wind,
    moisture,
    coeffs,
    damping,
    vmix,
    basis,
    edge_source,
    row_cell,
    col_cell,
    cond_rate,
    saturation,
    ancestry,
):
    levels = height.shape[1]
    size_x = height.shape[2]
    size_y = height.shape[3]
    full_x = row_cell.shape[0]
    full_y = col_cell.shape[0]
    rim_points = basis.shape[1]
    row_index = lax.axis_index("gx")
    col_index = lax.axis_index("gy")
    row_start = row_index * size_x
    col_start = col_index * size_y
    coeff_new = jnp.einsum("lj,mfjk->mflk", vmix, coeffs, precision=lax.Precision.HIGHEST) * damping
    coeff_low = coeff_new.astype(jnp.bfloat16).reshape(4 * levels, -1)
    rim_part = jnp.dot(coeff_low, basis, preferred_element_type=jnp.float32)
    rim = lax.psum(rim_part, ("gx", "gy"))
    western_edge = side_values(
        rim, lax.dynamic_slice_in_dim(edge_source, col_start, size_y), rim_points, levels
    )
    eastern_edge = side_values(
        rim, lax.dynamic_slice_in_dim(edge_source, full_y + col_start, size_y), rim_points, levels
    )
    southern_edge = side_values(
        rim,
        lax.dynamic_slice_in_dim(edge_source, 2 * full_y + row_start, size_x),
        rim_points,
        levels,
    )
    northern_edge = side_values(
        rim,
        lax.dynamic_slice_in_dim(edge_source, 2 * full_y + full_x + row_start, size_x),
        rim_points,
        levels,
    )
    sides = (western_edge, eastern_edge, southern_edge, northern_edge)
    flags = (
        row_index == 0,
        row_index == lax.axis_size("gx") - 1,
        col_index == 0,
        col_index == lax.axis_size("gy") - 1,
    )
    h_field = height[0]
    u_field = wind[0, 0]
    v_field = wind[0, 1]
    q_field = moisture[0]
    for substep in range(ACOUSTIC):
        h_pad = extended(h_field[None], (("gx", 2), ("gy", 3)), 1)
        h_pad = frame(h_pad, pick_sides(sides, 0, 1), flags)[0]
        u_field = u_field - acoustic_substep * (h_pad[:, 2:, 1:-1] - h_pad[:, :-2, 1:-1])
        v_field = v_field - acoustic_substep * (h_pad[:, 1:-1, 2:] - h_pad[:, 1:-1, :-2])
        wind_pad = extended(jnp.stack([u_field, v_field]), (("gx", 2), ("gy", 3)), 1)
        wind_pad = frame(wind_pad, pick_sides(sides, 1, 3), flags)
        u_pad = wind_pad[0]
        v_pad = wind_pad[1]
        h_field = h_field - acoustic_substep * (
            u_pad[:, 2:, 1:-1] - u_pad[:, :-2, 1:-1] + (v_pad[:, 1:-1, 2:] - v_pad[:, 1:-1, :-2])
        )
    q_pad = extended(q_field[None], (("gx", 2), ("gy", 3)), 1)
    q_pad = frame(q_pad, pick_sides(sides, 3, 4), flags)[0]
    flux = (
        jnp.maximum(u_field, 0.0) * (q_field - q_pad[:, :-2, 1:-1])
        + jnp.minimum(u_field, 0.0) * (q_pad[:, 2:, 1:-1] - q_field)
        + (
            jnp.maximum(v_field, 0.0) * (q_field - q_pad[:, 1:-1, :-2])
            + jnp.minimum(v_field, 0.0) * (q_pad[:, 1:-1, 2:] - q_field)
        )
    )
    q_field = q_field - drift_step * flux
    excess = jnp.maximum(q_field - saturation[:, None, None], 0.0)
    fallen = cond_rate[:, None, None] * excess
    q_field = q_field - fallen
    rain = jnp.sum(fallen, axis=0)
    coarse_rows = full_x // RATIO
    coarse_cols = full_y // RATIO
    row_table = (row_cell[None, :] == lax.iota(jnp.int32, coarse_rows)[:, None]).astype(jnp.float32)
    col_table = (col_cell[None, :] == lax.iota(jnp.int32, coarse_cols)[:, None]).astype(jnp.float32)
    row_count = jnp.sum(row_table, axis=1)
    col_count = jnp.sum(col_table, axis=1)
    local_rows = lax.dynamic_slice_in_dim(row_table, row_start, size_x, 1)
    local_cols = lax.dynamic_slice_in_dim(col_table, col_start, size_y, 1)
    partial_value = jnp.einsum("ax,lxy->lay", local_rows, q_field, precision=lax.Precision.HIGHEST)
    partial_value = jnp.einsum(
        "lay,by->lab", partial_value, local_cols, precision=lax.Precision.HIGHEST
    )
    sums = lax.psum(partial_value, "gy")
    sums = lax.psum(sums, "gx")
    coarse = sums / (row_count[:, None] * col_count[None, :])
    states = (
        h_field[None],
        jnp.stack([u_field, v_field])[None],
        q_field[None],
        rain[None],
        coarse[None],
        coeff_new,
    )
    member_here = lax.axis_index("mem")
    everyone = (
        lax.all_gather(states[0], "mem", axis=0, tiled=True),
        lax.all_gather(states[1], "mem", axis=0, tiled=True),
        lax.all_gather(states[2], "mem", axis=0, tiled=True),
        lax.all_gather(states[3], "mem", axis=0, tiled=True),
        lax.all_gather(states[4], "mem", axis=0, tiled=True),
        lax.all_gather(states[5], "mem", axis=0, tiled=True),
    )
    source = ancestry[member_here]
    cloned = tuple(
        (lax.dynamic_index_in_dim(whole, source, 0, keepdims=True) for whole in everyone)
    )
    return (cloned[0], cloned[1], cloned[2], cloned[3], cloned[4], cloned[5])


def solution(mesh):
    in_specs = (
        P("mem", None, "gx", "gy"),
        P("mem", None, None, "gx", "gy"),
        P("mem", None, "gx", "gy"),
        P("mem", None, None, ("gx", "gy")),
        P(("gx", "gy")),
        P(),
        P(("gx", "gy"), None),
        P(),
        P(),
        P(),
        P(),
        P(),
        P(),
    )
    out_specs = (
        P("mem", None, "gx", "gy"),
        P("mem", None, None, "gx", "gy"),
        P("mem", None, "gx", "gy"),
        P("mem", "gx", "gy"),
        P("mem", None, None, None),
        P("mem", None, None, ("gx", "gy")),
    )
    return jax.shard_map(body, mesh=mesh, in_specs=in_specs, out_specs=out_specs, check_vma=False)
```

profile of v0, /device:TPU:10, one launch (start us, length us, event | category | flops | bytes accessed | tf_op | source)
XLA Modules:
  0.0 245.4 jit_solution(11485259475965265100)
XLA Ops:
  1.5 1.7 collective-permute-start
  5.3 4.3 %collective-permute-start.16 = (f32[1,4,1,128]{3,1,2,0:T(4,128)S(1)}, f32[1,4,1,128]{3,1,2,0:T(4,128)S(1)}, u32[]{:S(2)}, u32[]{:S(2)}) collective-permute-start(f32[1,4,1,128]{3,1,2,0:T(4,128)S(1)} %copy.119), channel_id=1, source_target_pairs={{0,2},{2,4},{4,6},{1,3},{3,5},{5,7},{8,10},{10,12},{12,14},{9,11},... | collective-permute-start | bytes 6152 | tf_op jit(solution)/shard_map/ppermute | solution.py:17
  18.1 25.0 %psum.21 = f32[16,384]{1,0:T(8,128)S(1)} all-reduce(f32[16,384]{1,0:T(8,128)S(1)} %fusion.78), channel_id=1, replica_groups=mesh['mem'=4,'gx'=4,'gy'=2] {'gx','gy'}, use_global_device_ids=true, to_apply=%region_0.0 | all-reduce | flops 6144 | bytes 49152 | tf_op jit(solution)/shard_map/psum | solution.py:82
  44.0 16.5 %all_gather.23 = f32[4,4,4,2048]{3,2,1,0:T(4,128)S(1)} all-gather(f32[1,4,4,2048]{3,2,1,0:T(4,128)S(1)} %get-tuple-element.293), channel_id=1, replica_groups=mesh['mem'=4,'gx'=4,'gy'=2] {'mem'}, dimensions={0}, use_global_device_ids=true | all-gather | bytes 655360 | tf_op jit(solution)/shard_map/all_gather | solution.py:169
  63.0 3.3 %collective-permute-start.3 = (f32[1,4,34,1]{3,1,2,0:T(4,128)S(1)}, f32[1,4,34,1]{3,1,2,0:T(4,128)S(1)}, u32[]{:S(2)}, u32[]{:S(2)}) collective-permute-start(f32[1,4,34,1]{3,1,2,0:T(4,128)S(1)} %get-tuple-element.271), channel_id=1, source_target_pairs={{1,0},{3,2},{5,4},{7,6},{9,8},{11,10},{13,12},{15,14},{17,16},{19,... | collective-permute-start | bytes 1640 | tf_op jit(solution)/shard_map/ppermute | solution.py:20
  68.2 4.3 %collective-permute-done.2 = f32[1,4,34,1]{3,1,2,0:T(4,128)S(1)} collective-permute-done((f32[1,4,34,1]{3,1,2,0:T(4,128)S(1)}, f32[1,4,34,1]{3,1,2,0:T(4,128)S(1)}, u32[]{:S(2)}, u32[]{:S(2)}) %collective-permute-start.2) | collective-permute-done | bytes 576 | tf_op jit(solution)/shard_map/ppermute | solution.py:17
  75.2 2.4 scatter.71
  79.1 3.0 %collective-permute-start.4 = (f32[2,4,1,128]{3,1,2,0:T(4,128)S(1)}, f32[2,4,1,128]{3,1,2,0:T(4,128)S(1)}, u32[]{:S(2)}, u32[]{:S(2)}) collective-permute-start(f32[2,4,1,128]{3,1,2,0:T(4,128)S(1)} %get-tuple-element.262), channel_id=1, source_target_pairs={{0,2},{2,4},{4,6},{1,3},{3,5},{5,7},{8,10},{10,12},{12,14},{9,11},... | collective-permute-start | bytes 12296 | tf_op jit(solution)/shard_map/ppermute | solution.py:17
  82.3 1.6 collective-permute-start.19
  85.4 4.6 %collective-permute-start.7 = (f32[2,4,34,1]{3,1,2,0:T(4,128)S(1)}, f32[2,4,34,1]{3,1,2,0:T(4,128)S(1)}, u32[]{:S(2)}, u32[]{:S(2)}) collective-permute-start(f32[2,4,34,1]{3,1,2,0:T(4,128)S(1)} %get-tuple-element.257), channel_id=1, source_target_pairs={{1,0},{3,2},{5,4},{7,6},{9,8},{11,10},{13,12},{15,14},{17,16},{19,... | collective-permute-start | bytes 3272 | tf_op jit(solution)/shard_map/ppermute | solution.py:20
  91.2 2.6 %collective-permute-done.7 = f32[2,4,34,1]{3,1,2,0:T(4,128)S(1)} collective-permute-done((f32[2,4,34,1]{3,1,2,0:T(4,128)S(1)}, f32[2,4,34,1]{3,1,2,0:T(4,128)S(1)}, u32[]{:S(2)}, u32[]{:S(2)}) %collective-permute-start.7) | collective-permute-done | bytes 1120 | tf_op jit(solution)/shard_map/ppermute | solution.py:20
  93.8 4.4 %collective-permute-done.6 = f32[2,4,34,1]{3,1,2,0:T(4,128)S(1)} collective-permute-done((f32[2,4,34,1]{3,1,2,0:T(4,128)S(1)}, f32[2,4,34,1]{3,1,2,0:T(4,128)S(1)}, u32[]{:S(2)}, u32[]{:S(2)}) %collective-permute-start.6) | collective-permute-done | bytes 1120 | tf_op jit(solution)/shard_map/ppermute | solution.py:17
  98.5 1.6 scatter.74
  101.3 4.8 %scatter.79 = f32[2,4,34,130]{3,1,2,0:T(4,128)S(1)} dynamic-update-slice(f32[2,4,34,130]{3,1,2,0:T(4,128)S(1)} %scatter.76, f32[2,4,32,1]{3,1,2,0:T(4,128)S(1)} %slice_select_fusion.2, s32[]{:T(128)} %constant.509.clone.1, s32[]{:T(128)} %constant.509.clone.1, s32[]{:T(128)} %constant.516.clone.1, s32[]{:T(128)} %constant.522.clone.1) | dynamic-update-slice | bytes 2052 | tf_op jit(solution)/shard_map/scatter | solution.py:44
  106.3 1.9 collective-permute-start.8
  109.7 1.9 collective-permute-done.9
  116.0 3.4 %collective-permute-done.10 = f32[1,4,34,1]{3,1,2,0:T(4,128)S(1)} collective-permute-done((f32[1,4,34,1]{3,1,2,0:T(4,128)S(1)}, f32[1,4,34,1]{3,1,2,0:T(4,128)S(1)}, u32[]{:S(2)}, u32[]{:S(2)}) %collective-permute-start.10) | collective-permute-done | bytes 576 | tf_op jit(solution)/shard_map/ppermute | solution.py:17
  119.6 1.5 scatter.80
  123.2 2.4 scatter.99
  125.6 2.6 %scatter.85 = f32[4,34,130]{2,0,1:T(4,128)S(1)} dynamic-update-slice(f32[4,34,130]{2,0,1:T(4,128)S(1)} %bitcast.149, f32[4,32,1]{2,0,1:T(4,128)S(1)} %copy.88, s32[]{:T(128)} %constant.509.clone.1, s32[]{:T(128)} %constant.516.clone.1, s32[]{:T(128)} %constant.522.clone.1) | dynamic-update-slice | bytes 1028 | tf_op jit(solution)/shard_map/scatter | solution.py:44
  129.9 3.5 %collective-permute-start.12 = (f32[2,4,1,128]{3,1,2,0:T(4,128)S(1)}, f32[2,4,1,128]{3,1,2,0:T(4,128)S(1)}, u32[]{:S(2)}, u32[]{:S(2)}) collective-permute-start(f32[2,4,1,128]{3,1,2,0:T(4,128)S(1)} %get-tuple-element.260), channel_id=1, source_target_pairs={{0,2},{2,4},{4,6},{1,3},{3,5},{5,7},{8,10},{10,12},{12,14},{9,11},... | collective-permute-start | bytes 12296 | tf_op jit(solution)/shard_map/ppermute | solution.py:17
  133.4 16.1 %all-gather.1 = f32[8,4,32,128]{3,2,1,0:T(8,128)S(1)} all-gather(f32[2,4,32,128]{3,2,1,0:T(8,128)S(1)} %copy.92), channel_id=3, replica_groups=mesh['mem'=4,'gx'=4,'gy'=2] {'mem'}, dimensions={0}, use_global_device_ids=true | all-gather | bytes 655360 | tf_op jit(solution)/shard_map/all_gather | solution.py:165
  150.3 14.7 %all-gather.2 = f32[16,32,128]{2,1,0:T(8,128)S(1)} all-gather(f32[4,32,128]{2,1,0:T(8,128)S(1)} %copy.101), channel_id=4, replica_groups=mesh['mem'=4,'gx'=4,'gy'=2] {'mem'}, dimensions={0}, use_global_device_ids=true | all-gather | bytes 327680 | tf_op jit(solution)/shard_map/all_gather | solution.py:166
  165.7 13.2 %all-gather.3 = f32[128,128]{1,0:T(8,128)S(1)} all-gather(f32[32,128]{1,0:T(8,128)S(1)} %get-tuple-element.246), channel_id=5, replica_groups=mesh['mem'=4,'gx'=4,'gy'=2] {'mem'}, dimensions={0}, use_global_device_ids=true | all-gather | bytes 81920 | tf_op jit(solution)/shard_map/all_gather | solution.py:167
  179.2 7.0 %psum.22 = f32[4,16,32]{2,1,0:T(8,128)S(1)} all-reduce(f32[4,16,32]{2,1,0:T(8,128)S(1)} %fusion.36), channel_id=1, replica_groups=mesh['mem'=4,'gx'=4,'gy'=2] {'gy'}, use_global_device_ids=true, to_apply=%region_2.3 | all-reduce | flops 2048 | bytes 16384 | tf_op jit(solution)/shard_map/psum | solution.py:151
  186.2 10.3 %psum.23 = f32[4,16,32]{2,1,0:T(8,128)S(1)} all-reduce(f32[4,16,32]{2,1,0:T(8,128)S(1)} %psum.22), channel_id=1, replica_groups=mesh['mem'=4,'gx'=4,'gy'=2] {'gx'}, use_global_device_ids=true, to_apply=%region_3.4 | all-reduce | flops 2048 | bytes 16384 | tf_op jit(solution)/shard_map/psum | solution.py:152
  196.5 13.6 %all-gather.4 = f32[16,16,32]{2,1,0:T(8,128)S(1)} all-gather(f32[4,16,32]{2,1,0:T(8,128)S(1)} %broadcast_divide_fusion), channel_id=6, replica_groups=mesh['mem'=4,'gx'=4,'gy'=2] {'mem'}, dimensions={0}, use_global_device_ids=true | all-gather | bytes 40960 | tf_op jit(solution)/shard_map/all_gather | solution.py:168
  211.5 3.8 %collective-permute-start.15 = (f32[2,4,34,1]{3,1,2,0:T(4,128)S(1)}, f32[2,4,34,1]{3,1,2,0:T(4,128)S(1)}, u32[]{:S(2)}, u32[]{:S(2)}) collective-permute-start(f32[2,4,34,1]{3,1,2,0:T(4,128)S(1)} %get-tuple-element.255), channel_id=1, source_target_pairs={{1,0},{3,2},{5,4},{7,6},{9,8},{11,10},{13,12},{15,14},{17,16},{19,... | collective-permute-start | bytes 3272 | tf_op jit(solution)/shard_map/ppermute | solution.py:20
  217.9 4.4 %collective-permute-done.14 = f32[2,4,34,1]{3,1,2,0:T(4,128)S(1)} collective-permute-done((f32[2,4,34,1]{3,1,2,0:T(4,128)S(1)}, f32[2,4,34,1]{3,1,2,0:T(4,128)S(1)}, u32[]{:S(2)}, u32[]{:S(2)}) %collective-permute-start.14) | collective-permute-done | bytes 1120 | tf_op jit(solution)/shard_map/ppermute | solution.py:17
  222.5 1.6 scatter.86
  225.3 4.8 %scatter.91 = f32[2,4,34,130]{3,1,2,0:T(4,128)S(1)} dynamic-update-slice(f32[2,4,34,130]{3,1,2,0:T(4,128)S(1)} %scatter.90, f32[2,4,32,1]{3,1,2,0:T(4,128)S(1)} %slice_select_fusion, s32[]{:T(128)} %constant.509.clone.1, s32[]{:T(128)} %constant.509.clone.1, s32[]{:T(128)} %constant.516.clone.1, s32[]{:T(128)} %constant.522.clone.1) | dynamic-update-slice | bytes 2052 | tf_op jit(solution)/shard_map/scatter | solution.py:44
  230.3 14.4 %all-gather = f32[16,32,128]{2,1,0:T(8,128)S(1)} all-gather(f32[4,32,128]{2,1,0:T(8,128)S(1)} %copy.91), channel_id=2, replica_groups=mesh['mem'=4,'gx'=4,'gy'=2] {'mem'}, dimensions={0}, use_global_device_ids=true | all-gather | bytes 327680 | tf_op jit(solution)/shard_map/all_gather | solution.py:164
  (157 shorter events, 40.8 us)
Async XLA Ops:
  0.6 17.1 %copy-start = (bf16[2048,384]{1,0:T(8,128)(2,1)S(1)}, bf16[2048,384]{1,0:T(8,128)(2,1)}, u32[]{:S(2)}) copy-start(bf16[2048,384]{1,0:T(8,128)(2,1)} %param.59) | copy-start | bytes 4718596
  0.6 42.4 %copy-start.6 = (s32[768]{0:T(1024)S(1)}, s32[768]{0:T(1024)}, u32[]{:S(2)}) copy-start(s32[768]{0:T(1024)} %param.60) | copy-start | bytes 9220
  0.7 43.3 %copy-start.3 = (f32[1,2,4,32,128]{4,3,2,1,0:T(8,128)S(1)}, f32[1,2,4,32,128]{4,3,2,1,0:T(8,128)}, u32[]{:S(2)}) copy-start(f32[1,2,4,32,128]{4,3,2,1,0:T(8,128)} %param.54) | copy-start | bytes 393220
  1.5 61.3 %collective-permute-start = (f32[1,4,1,128]{3,1,2,0:T(4,128)S(1)}, f32[1,4,1,128]{3,1,2,0:T(4,128)S(1)}, u32[]{:S(2)}, u32[]{:S(2)}) collective-permute-start(f32[1,4,1,128]{3,1,2,0:T(4,128)S(1)} %copy.117), channel_id=1, source_target_pairs={{0,2},{2,4},{4,6},{1,3},{3,5},{5,7},{8,10},{10,12},{12,14},{9,11},... | collective-permute-start | bytes 6152 | tf_op jit(solution)/shard_map/ppermute | solution.py:17
  3.3 59.6 %collective-permute-start.1 = (f32[1,4,1,128]{3,1,2,0:T(4,128)S(1)}, f32[1,4,1,128]{3,1,2,0:T(4,128)S(1)}, u32[]{:S(2)}, u32[]{:S(2)}) collective-permute-start(f32[1,4,1,128]{3,1,2,0:T(4,128)S(1)} %copy.118), channel_id=1, source_target_pairs={{2,0},{4,2},{6,4},{3,1},{5,3},{7,5},{10,8},{12,10},{14,12},{11,9},... | collective-permute-start | bytes 6152 | tf_op jit(solution)/shard_map/ppermute | solution.py:20
  5.3 62.2 %collective-permute-start.16 = (f32[1,4,1,128]{3,1,2,0:T(4,128)S(1)}, f32[1,4,1,128]{3,1,2,0:T(4,128)S(1)}, u32[]{:S(2)}, u32[]{:S(2)}) collective-permute-start(f32[1,4,1,128]{3,1,2,0:T(4,128)S(1)} %copy.119), channel_id=1, source_target_pairs={{0,2},{2,4},{4,6},{1,3},{3,5},{5,7},{8,10},{10,12},{12,14},{9,11},... | collective-permute-start | bytes 6152 | tf_op jit(solution)/shard_map/ppermute | solution.py:17
  9.7 58.0 %collective-permute-start.17 = (f32[1,4,1,128]{3,1,2,0:T(4,128)S(1)}, f32[1,4,1,128]{3,1,2,0:T(4,128)S(1)}, u32[]{:S(2)}, u32[]{:S(2)}) collective-permute-start(f32[1,4,1,128]{3,1,2,0:T(4,128)S(1)} %copy.120), channel_id=1, source_target_pairs={{2,0},{4,2},{6,4},{3,1},{5,3},{7,5},{10,8},{12,10},{14,12},{11,9},... | collective-permute-start | bytes 6152 | tf_op jit(solution)/shard_map/ppermute | solution.py:20
  17.8 45.0 %copy-start.2 = (f32[1,4,32,128]{3,2,1,0:T(8,128)S(1)}, f32[1,4,32,128]{3,2,1,0:T(8,128)}, u32[]{:S(2)}) copy-start(f32[1,4,32,128]{3,2,1,0:T(8,128)} %param.53) | copy-start | bytes 196612
  17.8 49.8 %copy-start.1 = (f32[1,4,32,128]{3,2,1,0:T(8,128)S(1)}, f32[1,4,32,128]{3,2,1,0:T(8,128)}, u32[]{:S(2)}) copy-start(f32[1,4,32,128]{3,2,1,0:T(8,128)} %param.55) | copy-start | bytes 196612
  63.0 5.2 %collective-permute-start.3 = (f32[1,4,34,1]{3,1,2,0:T(4,128)S(1)}, f32[1,4,34,1]{3,1,2,0:T(4,128)S(1)}, u32[]{:S(2)}, u32[]{:S(2)}) collective-permute-start(f32[1,4,34,1]{3,1,2,0:T(4,128)S(1)} %get-tuple-element.271), channel_id=1, source_target_pairs={{1,0},{3,2},{5,4},{7,6},{9,8},{11,10},{13,12},{15,14},{17,16},{19,... | collective-permute-start | bytes 1640 | tf_op jit(solution)/shard_map/ppermute | solution.py:20
  66.3 6.2 %collective-permute-start.2 = (f32[1,4,34,1]{3,1,2,0:T(4,128)S(1)}, f32[1,4,34,1]{3,1,2,0:T(4,128)S(1)}, u32[]{:S(2)}, u32[]{:S(2)}) collective-permute-start(f32[1,4,34,1]{3,1,2,0:T(4,128)S(1)} %get-tuple-element.270), channel_id=1, source_target_pairs={{0,1},{2,3},{4,5},{6,7},{8,9},{10,11},{12,13},{14,15},{16,17},{18,... | collective-permute-start | bytes 1640 | tf_op jit(solution)/shard_map/ppermute | solution.py:17
  77.8 7.3 %collective-permute-start.5 = (f32[2,4,1,128]{3,1,2,0:T(4,128)S(1)}, f32[2,4,1,128]{3,1,2,0:T(4,128)S(1)}, u32[]{:S(2)}, u32[]{:S(2)}) collective-permute-start(f32[2,4,1,128]{3,1,2,0:T(4,128)S(1)} %get-tuple-element.263), channel_id=1, source_target_pairs={{2,0},{4,2},{6,4},{3,1},{5,3},{7,5},{10,8},{12,10},{14,12},{11,9},... | collective-permute-start | bytes 12296 | tf_op jit(solution)/shard_map/ppermute | solution.py:20
  79.1 6.0 %collective-permute-start.4 = (f32[2,4,1,128]{3,1,2,0:T(4,128)S(1)}, f32[2,4,1,128]{3,1,2,0:T(4,128)S(1)}, u32[]{:S(2)}, u32[]{:S(2)}) collective-permute-start(f32[2,4,1,128]{3,1,2,0:T(4,128)S(1)} %get-tuple-element.262), channel_id=1, source_target_pairs={{0,2},{2,4},{4,6},{1,3},{3,5},{5,7},{8,10},{10,12},{12,14},{9,11},... | collective-permute-start | bytes 12296 | tf_op jit(solution)/shard_map/ppermute | solution.py:17
  82.3 27.3 %collective-permute-start.19 = (f32[1,4,34,1]{3,1,2,0:T(4,128)S(1)}, f32[1,4,34,1]{3,1,2,0:T(4,128)S(1)}, u32[]{:S(2)}, u32[]{:S(2)}) collective-permute-start(f32[1,4,34,1]{3,1,2,0:T(4,128)S(1)} %get-tuple-element.267), channel_id=1, source_target_pairs={{1,0},{3,2},{5,4},{7,6},{9,8},{11,10},{13,12},{15,14},{17,16},{19,... | collective-permute-start | bytes 1640 | tf_op jit(solution)/shard_map/ppermute | solution.py:20
  83.9 25.7 %collective-permute-start.18 = (f32[1,4,34,1]{3,1,2,0:T(4,128)S(1)}, f32[1,4,34,1]{3,1,2,0:T(4,128)S(1)}, u32[]{:S(2)}, u32[]{:S(2)}) collective-permute-start(f32[1,4,34,1]{3,1,2,0:T(4,128)S(1)} %get-tuple-element.266), channel_id=1, source_target_pairs={{0,1},{2,3},{4,5},{6,7},{8,9},{10,11},{12,13},{14,15},{16,17},{18,... | collective-permute-start | bytes 1640 | tf_op jit(solution)/shard_map/ppermute | solution.py:17
  85.4 8.4 %collective-permute-start.7 = (f32[2,4,34,1]{3,1,2,0:T(4,128)S(1)}, f32[2,4,34,1]{3,1,2,0:T(4,128)S(1)}, u32[]{:S(2)}, u32[]{:S(2)}) collective-permute-start(f32[2,4,34,1]{3,1,2,0:T(4,128)S(1)} %get-tuple-element.257), channel_id=1, source_target_pairs={{1,0},{3,2},{5,4},{7,6},{9,8},{11,10},{13,12},{15,14},{17,16},{19,... | collective-permute-start | bytes 3272 | tf_op jit(solution)/shard_map/ppermute | solution.py:20
  89.9 8.3 %collective-permute-start.6 = (f32[2,4,34,1]{3,1,2,0:T(4,128)S(1)}, f32[2,4,34,1]{3,1,2,0:T(4,128)S(1)}, u32[]{:S(2)}, u32[]{:S(2)}) collective-permute-start(f32[2,4,34,1]{3,1,2,0:T(4,128)S(1)} %get-tuple-element.256), channel_id=1, source_target_pairs={{0,1},{2,3},{4,5},{6,7},{8,9},{10,11},{12,13},{14,15},{16,17},{18,... | collective-permute-start | bytes 3272 | tf_op jit(solution)/shard_map/ppermute | solution.py:17
  106.1 22.1 %copy-start.4 = (f32[4]{0:T(128)S(1)}, f32[4]{0:T(128)}, u32[]{:S(2)}) copy-start(f32[4]{0:T(128)} %param.64) | copy-start | bytes 52
  106.1 22.1 %copy-start.5 = (f32[4]{0:T(128)S(1)}, f32[4]{0:T(128)}, u32[]{:S(2)}) copy-start(f32[4]{0:T(128)} %param.63) | copy-start | bytes 52
  106.3 3.4 %collective-permute-start.8 = (f32[1,4,1,128]{3,1,2,0:T(4,128)S(1)}, f32[1,4,1,128]{3,1,2,0:T(4,128)S(1)}, u32[]{:S(2)}, u32[]{:S(2)}) collective-permute-start(f32[1,4,1,128]{3,1,2,0:T(4,128)S(1)} %get-tuple-element.274), channel_id=1, source_target_pairs={{0,2},{2,4},{4,6},{1,3},{3,5},{5,7},{8,10},{10,12},{12,14},{9,11},... | collective-permute-start | bytes 6152 | tf_op jit(solution)/shard_map/ppermute | solution.py:17
  108.2 3.4 %collective-permute-start.9 = (f32[1,4,1,128]{3,1,2,0:T(4,128)S(1)}, f32[1,4,1,128]{3,1,2,0:T(4,128)S(1)}, u32[]{:S(2)}, u32[]{:S(2)}) collective-permute-start(f32[1,4,1,128]{3,1,2,0:T(4,128)S(1)} %get-tuple-element.275), channel_id=1, source_target_pairs={{2,0},{4,2},{6,4},{3,1},{5,3},{7,5},{10,8},{12,10},{14,12},{11,9},... | collective-permute-start | bytes 6152 | tf_op jit(solution)/shard_map/ppermute | solution.py:20
  111.7 4.3 %collective-permute-start.11 = (f32[1,4,34,1]{3,1,2,0:T(4,128)S(1)}, f32[1,4,34,1]{3,1,2,0:T(4,128)S(1)}, u32[]{:S(2)}, u32[]{:S(2)}) collective-permute-start(f32[1,4,34,1]{3,1,2,0:T(4,128)S(1)} %get-tuple-element.269), channel_id=1, source_target_pairs={{1,0},{3,2},{5,4},{7,6},{9,8},{11,10},{13,12},{15,14},{17,16},{19,... | collective-permute-start | bytes 1640 | tf_op jit(solution)/shard_map/ppermute | solution.py:20
  113.2 6.2 %collective-permute-start.10 = (f32[1,4,34,1]{3,1,2,0:T(4,128)S(1)}, f32[1,4,34,1]{3,1,2,0:T(4,128)S(1)}, u32[]{:S(2)}, u32[]{:S(2)}) collective-permute-start(f32[1,4,34,1]{3,1,2,0:T(4,128)S(1)} %get-tuple-element.268), channel_id=1, source_target_pairs={{0,1},{2,3},{4,5},{6,7},{8,9},{10,11},{12,13},{14,15},{16,17},{18,... | collective-permute-start | bytes 1640 | tf_op jit(solution)/shard_map/ppermute | solution.py:17
  128.6 82.7 %collective-permute-start.13 = (f32[2,4,1,128]{3,1,2,0:T(4,128)S(1)}, f32[2,4,1,128]{3,1,2,0:T(4,128)S(1)}, u32[]{:S(2)}, u32[]{:S(2)}) collective-permute-start(f32[2,4,1,128]{3,1,2,0:T(4,128)S(1)} %get-tuple-element.261), channel_id=1, source_target_pairs={{2,0},{4,2},{6,4},{3,1},{5,3},{7,5},{10,8},{12,10},{14,12},{11,9},... | collective-permute-start | bytes 12296 | tf_op jit(solution)/shard_map/ppermute | solution.py:20
  129.9 81.4 %collective-permute-start.12 = (f32[2,4,1,128]{3,1,2,0:T(4,128)S(1)}, f32[2,4,1,128]{3,1,2,0:T(4,128)S(1)}, u32[]{:S(2)}, u32[]{:S(2)}) collective-permute-start(f32[2,4,1,128]{3,1,2,0:T(4,128)S(1)} %get-tuple-element.260), channel_id=1, source_target_pairs={{0,2},{2,4},{4,6},{1,3},{3,5},{5,7},{8,10},{10,12},{12,14},{9,11},... | collective-permute-start | bytes 12296 | tf_op jit(solution)/shard_map/ppermute | solution.py:17
  211.5 6.4 %collective-permute-start.15 = (f32[2,4,34,1]{3,1,2,0:T(4,128)S(1)}, f32[2,4,34,1]{3,1,2,0:T(4,128)S(1)}, u32[]{:S(2)}, u32[]{:S(2)}) collective-permute-start(f32[2,4,34,1]{3,1,2,0:T(4,128)S(1)} %get-tuple-element.255), channel_id=1, source_target_pairs={{1,0},{3,2},{5,4},{7,6},{9,8},{11,10},{13,12},{15,14},{17,16},{19,... | collective-permute-start | bytes 3272 | tf_op jit(solution)/shard_map/ppermute | solution.py:20
  215.3 6.9 %collective-permute-start.14 = (f32[2,4,34,1]{3,1,2,0:T(4,128)S(1)}, f32[2,4,34,1]{3,1,2,0:T(4,128)S(1)}, u32[]{:S(2)}, u32[]{:S(2)}) collective-permute-start(f32[2,4,34,1]{3,1,2,0:T(4,128)S(1)} %get-tuple-element.254), channel_id=1, source_target_pairs={{0,1},{2,3},{4,5},{6,7},{8,9},{10,11},{12,13},{14,15},{16,17},{18,... | collective-permute-start | bytes 3272 | tf_op jit(solution)/shard_map/ppermute | solution.py:17
where the time goes:
time: 246 us; the launch traced here: 245 us
  blocking collectives  131 us (53%)
  starting transfers between devices  42.1 us (17%)
  local copies, waits for them, and re-layouts  37.8 us (15%)
  waiting for transfers between devices  22.7 us (9%)
  other arithmetic  5.81 us (2%)
  between operations  3.52 us (1%)
  matrix products  2.68 us (1%)
    psum x1, blocking collectives, body(): rim = lax.psum(rim_part, ('gx', 'gy'))  25 us
    ppermute x10, starting transfers between devices, extended(): lax.ppermute(lax.slice_in_dim(block, 0, width, axis=dim), axis, backward)  21.2 us
    ppermute x10, starting transfers between devices, extended(): lax.ppermute(lax.slice_in_dim(block, block.shape[dim] - width, None, axis...  21 us
    scatter x5, local copies, waits for them, and re-layouts, frame(): padded.at[:, :, 1:1 + size_x, 1 + size_y]  16.9 us
    ppermute x10, waiting for transfers between devices, extended(): lax.ppermute(lax.slice_in_dim(block, block.shape[dim] - width, None, axis...  16.5 us
    all_gather x1, blocking collectives, body(): lax.all_gather(states[5], 'mem', axis=0, tiled=True)  16.5 us
    all_gather x1, blocking collectives, body(): lax.all_gather(states[1], 'mem', axis=0, tiled=True)  16.1 us
    all_gather x1, blocking collectives, body(): lax.all_gather(states[2], 'mem', axis=0, tiled=True)  14.7 us
  transfers between devices with their start and end apart: 20, of which 8 were waited for; matrix products, arithmetic and copies ran while one was open for 9% of the time, Pallas kernels for 0%

commit v1 on v0

--- a/solution.py
+++ b/solution.py
@@ -2,6 +2,7 @@
 import jax.numpy as jnp
 from jax import lax
 from jax.sharding import PartitionSpec as P
+from jax.lax import all_gather
 
 RATIO = 8
 ACOUSTIC = 2
@@ -79,7 +80,7 @@
     coeff_new = jnp.einsum("lj,mfjk->mflk", vmix, coeffs, precision=lax.Precision.HIGHEST) * damping
     coeff_low = coeff_new.astype(jnp.bfloat16).reshape(4 * levels, -1)
     rim_part = jnp.dot(coeff_low, basis, preferred_element_type=jnp.float32)
-    rim = lax.psum(rim_part, ("gx", "gy"))
+    rim = jnp.sum(all_gather(rim_part, ("gx", "gy")), axis=0)
     western_edge = side_values(
         rim, lax.dynamic_slice_in_dim(edge_source, col_start, size_y), rim_points, levels
     )

time: 246 us -> 238 us (0.967)
  blocking collectives: 131 us -> 122 us
    psum x1 -> x0, blocking collectives: 25 us -> none  [body(): rim = lax.psum(rim_part, ('gx', 'gy'))]
    all_gather x0 -> x1, blocking collectives: none -> 17.2 us  [body(): rim = jnp.sum(all_gather(rim_part, ('gx', 'gy')), axis=0)]
where the time goes in v1:
time: 238 us; the launch traced here: 237 us
  blocking collectives  122 us (51%)
  starting transfers between devices  42.3 us (18%)
  local copies, waits for them, and re-layouts  37.8 us (16%)
  waiting for transfers between devices  22.7 us (10%)
  other arithmetic  5.82 us (2%)
  between operations  3.53 us (1%)
  matrix products  2.68 us (1%)
    ppermute x10, starting transfers between devices, extended(): lax.ppermute(lax.slice_in_dim(block, 0, width, axis=dim), axis, backward)  21.5 us
    ppermute x10, starting transfers between devices, extended(): lax.ppermute(lax.slice_in_dim(block, block.shape[dim] - width, None, axis...  20.7 us
    all_gather x1, blocking collectives, body(): rim = jnp.sum(all_gather(rim_part, ('gx', 'gy')), axis=0)  17.2 us
    scatter x5, local copies, waits for them, and re-layouts, frame(): padded.at[:, :, 1:1 + size_x, 1 + size_y]  16.9 us
    ppermute x10, waiting for transfers between devices, extended(): lax.ppermute(lax.slice_in_dim(block, block.shape[dim] - width, None, axis...  16.2 us
    all_gather x1, blocking collectives, body(): lax.all_gather(states[1], 'mem', axis=0, tiled=True)  16.1 us
    all_gather x1, blocking collectives, body(): lax.all_gather(states[5], 'mem', axis=0, tiled=True)  15.8 us
    all_gather x1, blocking collectives, body(): lax.all_gather(states[2], 'mem', axis=0, tiled=True)  14.7 us
  transfers between devices with their start and end apart: 20, of which 8 were waited for; matrix products, arithmetic and copies ran while one was open for 9% of the time, Pallas kernels for 0%

profile of v1, /device:TPU:10, one launch (start us, length us, event | category | flops | bytes accessed | tf_op | source)
XLA Modules:
  0.0 237.1 jit_solution(6143085697636917998)
XLA Ops:
  1.5 1.7 collective-permute-start
  5.3 4.3 %collective-permute-start.16 = (f32[1,4,1,128]{3,1,2,0:T(4,128)S(1)}, f32[1,4,1,128]{3,1,2,0:T(4,128)S(1)}, u32[]{:S(2)}, u32[]{:S(2)}) collective-permute-start(f32[1,4,1,128]{3,1,2,0:T(4,128)S(1)} %copy.119), channel_id=1, source_target_pairs={{0,2},{2,4},{4,6},{1,3},{3,5},{5,7},{8,10},{10,12},{12,14},{9,11},... | collective-permute-start | bytes 6152 | tf_op jit(solution)/shard_map/ppermute | solution.py:18
  18.1 17.2 %all-gather = f32[128,384]{1,0:T(8,128)S(1)} all-gather(f32[16,384]{1,0:T(8,128)S(1)} %fusion.78), channel_id=2, replica_groups=mesh['mem'=4,'gx'=4,'gy'=2] {'gx','gy'}, dimensions={0}, use_global_device_ids=true | all-gather | bytes 221184 | tf_op jit(solution)/shard_map/all_gather | solution.py:83
  36.2 15.8 %all_gather.31 = f32[4,4,4,2048]{3,2,1,0:T(4,128)S(1)} all-gather(f32[1,4,4,2048]{3,2,1,0:T(4,128)S(1)} %get-tuple-element.293), channel_id=1, replica_groups=mesh['mem'=4,'gx'=4,'gy'=2] {'mem'}, dimensions={0}, use_global_device_ids=true | all-gather | bytes 655360 | tf_op jit(solution)/shard_map/all_gather | solution.py:170
  54.6 3.6 %collective-permute-start.3 = (f32[1,4,34,1]{3,1,2,0:T(4,128)S(1)}, f32[1,4,34,1]{3,1,2,0:T(4,128)S(1)}, u32[]{:S(2)}, u32[]{:S(2)}) collective-permute-start(f32[1,4,34,1]{3,1,2,0:T(4,128)S(1)} %get-tuple-element.271), channel_id=1, source_target_pairs={{1,0},{3,2},{5,4},{7,6},{9,8},{11,10},{13,12},{15,14},{17,16},{19,... | collective-permute-start | bytes 1640 | tf_op jit(solution)/shard_map/ppermute | solution.py:21
  60.2 4.3 %collective-permute-done.2 = f32[1,4,34,1]{3,1,2,0:T(4,128)S(1)} collective-permute-done((f32[1,4,34,1]{3,1,2,0:T(4,128)S(1)}, f32[1,4,34,1]{3,1,2,0:T(4,128)S(1)}, u32[]{:S(2)}, u32[]{:S(2)}) %collective-permute-start.2) | collective-permute-done | bytes 576 | tf_op jit(solution)/shard_map/ppermute | solution.py:18
  64.6 1.5 scatter.66
  67.2 2.4 %scatter.71 = f32[4,34,130]{2,0,1:T(4,128)S(1)} dynamic-update-slice(f32[4,34,130]{2,0,1:T(4,128)S(1)} %bitcast.151, f32[4,32,1]{2,0,1:T(4,128)S(1)} %copy.81, s32[]{:T(128)} %constant.509.clone.1, s32[]{:T(128)} %constant.517.clone.1, s32[]{:T(128)} %constant.523.clone.1) | dynamic-update-slice | bytes 1028 | tf_op jit(solution)/shard_map/scatter | solution.py:45
  71.1 3.0 %collective-permute-start.4 = (f32[2,4,1,128]{3,1,2,0:T(4,128)S(1)}, f32[2,4,1,128]{3,1,2,0:T(4,128)S(1)}, u32[]{:S(2)}, u32[]{:S(2)}) collective-permute-start(f32[2,4,1,128]{3,1,2,0:T(4,128)S(1)} %get-tuple-element.262), channel_id=1, source_target_pairs={{0,2},{2,4},{4,6},{1,3},{3,5},{5,7},{8,10},{10,12},{12,14},{9,11},... | collective-permute-start | bytes 12296 | tf_op jit(solution)/shard_map/ppermute | solution.py:18
  74.2 1.6 collective-permute-start.19
  77.3 4.6 %collective-permute-start.7 = (f32[2,4,34,1]{3,1,2,0:T(4,128)S(1)}, f32[2,4,34,1]{3,1,2,0:T(4,128)S(1)}, u32[]{:S(2)}, u32[]{:S(2)}) collective-permute-start(f32[2,4,34,1]{3,1,2,0:T(4,128)S(1)} %get-tuple-element.257), channel_id=1, source_target_pairs={{1,0},{3,2},{5,4},{7,6},{9,8},{11,10},{13,12},{15,14},{17,16},{19,... | collective-permute-start | bytes 3272 | tf_op jit(solution)/shard_map/ppermute | solution.py:21
  83.2 2.6 %collective-permute-done.7 = f32[2,4,34,1]{3,1,2,0:T(4,128)S(1)} collective-permute-done((f32[2,4,34,1]{3,1,2,0:T(4,128)S(1)}, f32[2,4,34,1]{3,1,2,0:T(4,128)S(1)}, u32[]{:S(2)}, u32[]{:S(2)}) %collective-permute-start.7) | collective-permute-done | bytes 1120 | tf_op jit(solution)/shard_map/ppermute | solution.py:21
  85.8 4.1 %collective-permute-done.6 = f32[2,4,34,1]{3,1,2,0:T(4,128)S(1)} collective-permute-done((f32[2,4,34,1]{3,1,2,0:T(4,128)S(1)}, f32[2,4,34,1]{3,1,2,0:T(4,128)S(1)}, u32[]{:S(2)}, u32[]{:S(2)}) %collective-permute-start.6) | collective-permute-done | bytes 1120 | tf_op jit(solution)/shard_map/ppermute | solution.py:18
  90.2 1.6 scatter.74
  93.0 4.8 %scatter.79 = f32[2,4,34,130]{3,1,2,0:T(4,128)S(1)} dynamic-update-slice(f32[2,4,34,130]{3,1,2,0:T(4,128)S(1)} %scatter.76, f32[2,4,32,1]{3,1,2,0:T(4,128)S(1)} %slice_select_fusion.2, s32[]{:T(128)} %constant.509.clone.1, s32[]{:T(128)} %constant.509.clone.1, s32[]{:T(128)} %constant.517.clone.1, s32[]{:T(128)} %constant.523.clone.1) | dynamic-update-slice | bytes 2052 | tf_op jit(solution)/shard_map/scatter | solution.py:45
  98.0 1.6 collective-permute-start.8
  101.2 2.1 collective-permute-done.9
  107.7 3.4 %collective-permute-done.10 = f32[1,4,34,1]{3,1,2,0:T(4,128)S(1)} collective-permute-done((f32[1,4,34,1]{3,1,2,0:T(4,128)S(1)}, f32[1,4,34,1]{3,1,2,0:T(4,128)S(1)}, u32[]{:S(2)}, u32[]{:S(2)}) %collective-permute-start.10) | collective-permute-done | bytes 576 | tf_op jit(solution)/shard_map/ppermute | solution.py:18
  114.9 2.4 %scatter.99 = f32[4,34,130]{2,0,1:T(4,128)S(1)} dynamic-update-slice(f32[4,34,130]{2,0,1:T(4,128)S(1)} %bitcast.149, f32[4,32,1]{2,0,1:T(4,128)S(1)} %copy.100, s32[]{:T(128)} %constant.509.clone.1, s32[]{:T(128)} %constant.517.clone.1, s32[]{:T(128)} %constant.523.clone.1) | dynamic-update-slice | bytes 1028 | tf_op jit(solution)/shard_map/scatter | solution.py:45
  117.3 2.6 %scatter.85 = f32[4,34,130]{2,0,1:T(4,128)S(1)} dynamic-update-slice(f32[4,34,130]{2,0,1:T(4,128)S(1)} %bitcast.150, f32[4,32,1]{2,0,1:T(4,128)S(1)} %copy.88, s32[]{:T(128)} %constant.509.clone.1, s32[]{:T(128)} %constant.517.clone.1, s32[]{:T(128)} %constant.523.clone.1) | dynamic-update-slice | bytes 1028 | tf_op jit(solution)/shard_map/scatter | solution.py:45
  121.6 3.5 %collective-permute-start.12 = (f32[2,4,1,128]{3,1,2,0:T(4,128)S(1)}, f32[2,4,1,128]{3,1,2,0:T(4,128)S(1)}, u32[]{:S(2)}, u32[]{:S(2)}) collective-permute-start(f32[2,4,1,128]{3,1,2,0:T(4,128)S(1)} %get-tuple-element.260), channel_id=1, source_target_pairs={{0,2},{2,4},{4,6},{1,3},{3,5},{5,7},{8,10},{10,12},{12,14},{9,11},... | collective-permute-start | bytes 12296 | tf_op jit(solution)/shard_map/ppermute | solution.py:18
  125.1 16.1 %all-gather.2 = f32[8,4,32,128]{3,2,1,0:T(8,128)S(1)} all-gather(f32[2,4,32,128]{3,2,1,0:T(8,128)S(1)} %copy.92), channel_id=4, replica_groups=mesh['mem'=4,'gx'=4,'gy'=2] {'mem'}, dimensions={0}, use_global_device_ids=true | all-gather | bytes 655360 | tf_op jit(solution)/shard_map/all_gather | solution.py:166
  142.0 14.7 %all-gather.3 = f32[16,32,128]{2,1,0:T(8,128)S(1)} all-gather(f32[4,32,128]{2,1,0:T(8,128)S(1)} %copy.101), channel_id=5, replica_groups=mesh['mem'=4,'gx'=4,'gy'=2] {'mem'}, dimensions={0}, use_global_device_ids=true | all-gather | bytes 327680 | tf_op jit(solution)/shard_map/all_gather | solution.py:167
  157.4 13.2 %all-gather.4 = f32[128,128]{1,0:T(8,128)S(1)} all-gather(f32[32,128]{1,0:T(8,128)S(1)} %get-tuple-element.246), channel_id=6, replica_groups=mesh['mem'=4,'gx'=4,'gy'=2] {'mem'}, dimensions={0}, use_global_device_ids=true | all-gather | bytes 81920 | tf_op jit(solution)/shard_map/all_gather | solution.py:168
  170.9 7.0 %psum.14 = f32[4,16,32]{2,1,0:T(8,128)S(1)} all-reduce(f32[4,16,32]{2,1,0:T(8,128)S(1)} %fusion.36), channel_id=1, replica_groups=mesh['mem'=4,'gx'=4,'gy'=2] {'gy'}, use_global_device_ids=true, to_apply=%region_2.3 | all-reduce | flops 2048 | bytes 16384 | tf_op jit(solution)/shard_map/psum | solution.py:152
  177.9 10.3 %psum.15 = f32[4,16,32]{2,1,0:T(8,128)S(1)} all-reduce(f32[4,16,32]{2,1,0:T(8,128)S(1)} %psum.14), channel_id=1, replica_groups=mesh['mem'=4,'gx'=4,'gy'=2] {'gx'}, use_global_device_ids=true, to_apply=%region_3.4 | all-reduce | flops 2048 | bytes 16384 | tf_op jit(solution)/shard_map/psum | solution.py:153
  188.2 13.6 %all-gather.5 = f32[16,16,32]{2,1,0:T(8,128)S(1)} all-gather(f32[4,16,32]{2,1,0:T(8,128)S(1)} %broadcast_divide_fusion), channel_id=7, replica_groups=mesh['mem'=4,'gx'=4,'gy'=2] {'mem'}, dimensions={0}, use_global_device_ids=true | all-gather | bytes 40960 | tf_op jit(solution)/shard_map/all_gather | solution.py:169
  203.2 3.8 %collective-permute-start.15 = (f32[2,4,34,1]{3,1,2,0:T(4,128)S(1)}, f32[2,4,34,1]{3,1,2,0:T(4,128)S(1)}, u32[]{:S(2)}, u32[]{:S(2)}) collective-permute-start(f32[2,4,34,1]{3,1,2,0:T(4,128)S(1)} %get-tuple-element.255), channel_id=1, source_target_pairs={{1,0},{3,2},{5,4},{7,6},{9,8},{11,10},{13,12},{15,14},{17,16},{19,... | collective-permute-start | bytes 3272 | tf_op jit(solution)/shard_map/ppermute | solution.py:21
  209.6 4.4 %collective-permute-done.14 = f32[2,4,34,1]{3,1,2,0:T(4,128)S(1)} collective-permute-done((f32[2,4,34,1]{3,1,2,0:T(4,128)S(1)}, f32[2,4,34,1]{3,1,2,0:T(4,128)S(1)}, u32[]{:S(2)}, u32[]{:S(2)}) %collective-permute-start.14) | collective-permute-done | bytes 1120 | tf_op jit(solution)/shard_map/ppermute | solution.py:18
  214.2 1.6 scatter.86
  217.0 4.8 %scatter.91 = f32[2,4,34,130]{3,1,2,0:T(4,128)S(1)} dynamic-update-slice(f32[2,4,34,130]{3,1,2,0:T(4,128)S(1)} %scatter.90, f32[2,4,32,1]{3,1,2,0:T(4,128)S(1)} %slice_select_fusion, s32[]{:T(128)} %constant.509.clone.1, s32[]{:T(128)} %constant.509.clone.1, s32[]{:T(128)} %constant.517.clone.1, s32[]{:T(128)} %constant.523.clone.1) | dynamic-update-slice | bytes 2052 | tf_op jit(solution)/shard_map/scatter | solution.py:45
  222.0 14.4 %all-gather.1 = f32[16,32,128]{2,1,0:T(8,128)S(1)} all-gather(f32[4,32,128]{2,1,0:T(8,128)S(1)} %copy.91), channel_id=3, replica_groups=mesh['mem'=4,'gx'=4,'gy'=2] {'mem'}, dimensions={0}, use_global_device_ids=true | all-gather | bytes 327680 | tf_op jit(solution)/shard_map/all_gather | solution.py:165
  (158 shorter events, 40.8 us)
Async XLA Ops:
  0.6 17.1 %copy-start = (bf16[2048,384]{1,0:T(8,128)(2,1)S(1)}, bf16[2048,384]{1,0:T(8,128)(2,1)}, u32[]{:S(2)}) copy-start(bf16[2048,384]{1,0:T(8,128)(2,1)} %param.59) | copy-start | bytes 4718596
  0.6 34.6 %copy-start.6 = (s32[768]{0:T(1024)S(1)}, s32[768]{0:T(1024)}, u32[]{:S(2)}) copy-start(s32[768]{0:T(1024)} %param.60) | copy-start | bytes 9220
  0.7 35.6 %copy-start.3 = (f32[1,2,4,32,128]{4,3,2,1,0:T(8,128)S(1)}, f32[1,2,4,32,128]{4,3,2,1,0:T(8,128)}, u32[]{:S(2)}) copy-start(f32[1,2,4,32,128]{4,3,2,1,0:T(8,128)} %param.54) | copy-start | bytes 393220
  1.5 52.8 %collective-permute-start = (f32[1,4,1,128]{3,1,2,0:T(4,128)S(1)}, f32[1,4,1,128]{3,1,2,0:T(4,128)S(1)}, u32[]{:S(2)}, u32[]{:S(2)}) collective-permute-start(f32[1,4,1,128]{3,1,2,0:T(4,128)S(1)} %copy.117), channel_id=1, source_target_pairs={{0,2},{2,4},{4,6},{1,3},{3,5},{5,7},{8,10},{10,12},{12,14},{9,11},... | collective-permute-start | bytes 6152 | tf_op jit(solution)/shard_map/ppermute | solution.py:18
  3.3 51.2 %collective-permute-start.1 = (f32[1,4,1,128]{3,1,2,0:T(4,128)S(1)}, f32[1,4,1,128]{3,1,2,0:T(4,128)S(1)}, u32[]{:S(2)}, u32[]{:S(2)}) collective-permute-start(f32[1,4,1,128]{3,1,2,0:T(4,128)S(1)} %copy.118), channel_id=1, source_target_pairs={{2,0},{4,2},{6,4},{3,1},{5,3},{7,5},{10,8},{12,10},{14,12},{11,9},... | collective-permute-start | bytes 6152 | tf_op jit(solution)/shard_map/ppermute | solution.py:21
  5.3 54.2 %collective-permute-start.16 = (f32[1,4,1,128]{3,1,2,0:T(4,128)S(1)}, f32[1,4,1,128]{3,1,2,0:T(4,128)S(1)}, u32[]{:S(2)}, u32[]{:S(2)}) collective-permute-start(f32[1,4,1,128]{3,1,2,0:T(4,128)S(1)} %copy.119), channel_id=1, source_target_pairs={{0,2},{2,4},{4,6},{1,3},{3,5},{5,7},{8,10},{10,12},{12,14},{9,11},... | collective-permute-start | bytes 6152 | tf_op jit(solution)/shard_map/ppermute | solution.py:18
  9.7 50.0 %collective-permute-start.17 = (f32[1,4,1,128]{3,1,2,0:T(4,128)S(1)}, f32[1,4,1,128]{3,1,2,0:T(4,128)S(1)}, u32[]{:S(2)}, u32[]{:S(2)}) collective-permute-start(f32[1,4,1,128]{3,1,2,0:T(4,128)S(1)} %copy.120), channel_id=1, source_target_pairs={{2,0},{4,2},{6,4},{3,1},{5,3},{7,5},{10,8},{12,10},{14,12},{11,9},... | collective-permute-start | bytes 6152 | tf_op jit(solution)/shard_map/ppermute | solution.py:21
  17.8 36.6 %copy-start.2 = (f32[1,4,32,128]{3,2,1,0:T(8,128)S(1)}, f32[1,4,32,128]{3,2,1,0:T(8,128)}, u32[]{:S(2)}) copy-start(f32[1,4,32,128]{3,2,1,0:T(8,128)} %param.53) | copy-start | bytes 196612
  18.1 41.5 %copy-start.1 = (f32[1,4,32,128]{3,2,1,0:T(8,128)S(1)}, f32[1,4,32,128]{3,2,1,0:T(8,128)}, u32[]{:S(2)}) copy-start(f32[1,4,32,128]{3,2,1,0:T(8,128)} %param.55) | copy-start | bytes 196612
  54.6 5.6 %collective-permute-start.3 = (f32[1,4,34,1]{3,1,2,0:T(4,128)S(1)}, f32[1,4,34,1]{3,1,2,0:T(4,128)S(1)}, u32[]{:S(2)}, u32[]{:S(2)}) collective-permute-start(f32[1,4,34,1]{3,1,2,0:T(4,128)S(1)} %get-tuple-element.271), channel_id=1, source_target_pairs={{1,0},{3,2},{5,4},{7,6},{9,8},{11,10},{13,12},{15,14},{17,16},{19,... | collective-permute-start | bytes 1640 | tf_op jit(solution)/shard_map/ppermute | solution.py:21
  58.2 6.2 %collective-permute-start.2 = (f32[1,4,34,1]{3,1,2,0:T(4,128)S(1)}, f32[1,4,34,1]{3,1,2,0:T(4,128)S(1)}, u32[]{:S(2)}, u32[]{:S(2)}) collective-permute-start(f32[1,4,34,1]{3,1,2,0:T(4,128)S(1)} %get-tuple-element.270), channel_id=1, source_target_pairs={{0,1},{2,3},{4,5},{6,7},{8,9},{10,11},{12,13},{14,15},{16,17},{18,... | collective-permute-start | bytes 1640 | tf_op jit(solution)/shard_map/ppermute | solution.py:18
  69.8 7.3 %collective-permute-start.5 = (f32[2,4,1,128]{3,1,2,0:T(4,128)S(1)}, f32[2,4,1,128]{3,1,2,0:T(4,128)S(1)}, u32[]{:S(2)}, u32[]{:S(2)}) collective-permute-start(f32[2,4,1,128]{3,1,2,0:T(4,128)S(1)} %get-tuple-element.263), channel_id=1, source_target_pairs={{2,0},{4,2},{6,4},{3,1},{5,3},{7,5},{10,8},{12,10},{14,12},{11,9},... | collective-permute-start | bytes 12296 | tf_op jit(solution)/shard_map/ppermute | solution.py:21
  71.1 6.0 %collective-permute-start.4 = (f32[2,4,1,128]{3,1,2,0:T(4,128)S(1)}, f32[2,4,1,128]{3,1,2,0:T(4,128)S(1)}, u32[]{:S(2)}, u32[]{:S(2)}) collective-permute-start(f32[2,4,1,128]{3,1,2,0:T(4,128)S(1)} %get-tuple-element.262), channel_id=1, source_target_pairs={{0,2},{2,4},{4,6},{1,3},{3,5},{5,7},{8,10},{10,12},{12,14},{9,11},... | collective-permute-start | bytes 12296 | tf_op jit(solution)/shard_map/ppermute | solution.py:18
  74.2 26.7 %collective-permute-start.19 = (f32[1,4,34,1]{3,1,2,0:T(4,128)S(1)}, f32[1,4,34,1]{3,1,2,0:T(4,128)S(1)}, u32[]{:S(2)}, u32[]{:S(2)}) collective-permute-start(f32[1,4,34,1]{3,1,2,0:T(4,128)S(1)} %get-tuple-element.267), channel_id=1, source_target_pairs={{1,0},{3,2},{5,4},{7,6},{9,8},{11,10},{13,12},{15,14},{17,16},{19,... | collective-permute-start | bytes 1640 | tf_op jit(solution)/shard_map/ppermute | solution.py:21
  75.8 25.2 %collective-permute-start.18 = (f32[1,4,34,1]{3,1,2,0:T(4,128)S(1)}, f32[1,4,34,1]{3,1,2,0:T(4,128)S(1)}, u32[]{:S(2)}, u32[]{:S(2)}) collective-permute-start(f32[1,4,34,1]{3,1,2,0:T(4,128)S(1)} %get-tuple-element.266), channel_id=1, source_target_pairs={{0,1},{2,3},{4,5},{6,7},{8,9},{10,11},{12,13},{14,15},{16,17},{18,... | collective-permute-start | bytes 1640 | tf_op jit(solution)/shard_map/ppermute | solution.py:18
  77.3 8.5 %collective-permute-start.7 = (f32[2,4,34,1]{3,1,2,0:T(4,128)S(1)}, f32[2,4,34,1]{3,1,2,0:T(4,128)S(1)}, u32[]{:S(2)}, u32[]{:S(2)}) collective-permute-start(f32[2,4,34,1]{3,1,2,0:T(4,128)S(1)} %get-tuple-element.257), channel_id=1, source_target_pairs={{1,0},{3,2},{5,4},{7,6},{9,8},{11,10},{13,12},{15,14},{17,16},{19,... | collective-permute-start | bytes 3272 | tf_op jit(solution)/shard_map/ppermute | solution.py:21
  81.9 8.1 %collective-permute-start.6 = (f32[2,4,34,1]{3,1,2,0:T(4,128)S(1)}, f32[2,4,34,1]{3,1,2,0:T(4,128)S(1)}, u32[]{:S(2)}, u32[]{:S(2)}) collective-permute-start(f32[2,4,34,1]{3,1,2,0:T(4,128)S(1)} %get-tuple-element.256), channel_id=1, source_target_pairs={{0,1},{2,3},{4,5},{6,7},{8,9},{10,11},{12,13},{14,15},{16,17},{18,... | collective-permute-start | bytes 3272 | tf_op jit(solution)/shard_map/ppermute | solution.py:18
  97.8 22.1 %copy-start.4 = (f32[4]{0:T(128)S(1)}, f32[4]{0:T(128)}, u32[]{:S(2)}) copy-start(f32[4]{0:T(128)} %param.64) | copy-start | bytes 52
  97.8 22.1 %copy-start.5 = (f32[4]{0:T(128)S(1)}, f32[4]{0:T(128)}, u32[]{:S(2)}) copy-start(f32[4]{0:T(128)} %param.63) | copy-start | bytes 52
  98.0 3.1 %collective-permute-start.8 = (f32[1,4,1,128]{3,1,2,0:T(4,128)S(1)}, f32[1,4,1,128]{3,1,2,0:T(4,128)S(1)}, u32[]{:S(2)}, u32[]{:S(2)}) collective-permute-start(f32[1,4,1,128]{3,1,2,0:T(4,128)S(1)} %get-tuple-element.274), channel_id=1, source_target_pairs={{0,2},{2,4},{4,6},{1,3},{3,5},{5,7},{8,10},{10,12},{12,14},{9,11},... | collective-permute-start | bytes 6152 | tf_op jit(solution)/shard_map/ppermute | solution.py:18
  99.7 3.6 %collective-permute-start.9 = (f32[1,4,1,128]{3,1,2,0:T(4,128)S(1)}, f32[1,4,1,128]{3,1,2,0:T(4,128)S(1)}, u32[]{:S(2)}, u32[]{:S(2)}) collective-permute-start(f32[1,4,1,128]{3,1,2,0:T(4,128)S(1)} %get-tuple-element.275), channel_id=1, source_target_pairs={{2,0},{4,2},{6,4},{3,1},{5,3},{7,5},{10,8},{12,10},{14,12},{11,9},... | collective-permute-start | bytes 6152 | tf_op jit(solution)/shard_map/ppermute | solution.py:21
  103.4 4.3 %collective-permute-start.11 = (f32[1,4,34,1]{3,1,2,0:T(4,128)S(1)}, f32[1,4,34,1]{3,1,2,0:T(4,128)S(1)}, u32[]{:S(2)}, u32[]{:S(2)}) collective-permute-start(f32[1,4,34,1]{3,1,2,0:T(4,128)S(1)} %get-tuple-element.269), channel_id=1, source_target_pairs={{1,0},{3,2},{5,4},{7,6},{9,8},{11,10},{13,12},{15,14},{17,16},{19,... | collective-permute-start | bytes 1640 | tf_op jit(solution)/shard_map/ppermute | solution.py:21
  104.9 6.2 %collective-permute-start.10 = (f32[1,4,34,1]{3,1,2,0:T(4,128)S(1)}, f32[1,4,34,1]{3,1,2,0:T(4,128)S(1)}, u32[]{:S(2)}, u32[]{:S(2)}) collective-permute-start(f32[1,4,34,1]{3,1,2,0:T(4,128)S(1)} %get-tuple-element.268), channel_id=1, source_target_pairs={{0,1},{2,3},{4,5},{6,7},{8,9},{10,11},{12,13},{14,15},{16,17},{18,... | collective-permute-start | bytes 1640 | tf_op jit(solution)/shard_map/ppermute | solution.py:18
  120.3 82.7 %collective-permute-start.13 = (f32[2,4,1,128]{3,1,2,0:T(4,128)S(1)}, f32[2,4,1,128]{3,1,2,0:T(4,128)S(1)}, u32[]{:S(2)}, u32[]{:S(2)}) collective-permute-start(f32[2,4,1,128]{3,1,2,0:T(4,128)S(1)} %get-tuple-element.261), channel_id=1, source_target_pairs={{2,0},{4,2},{6,4},{3,1},{5,3},{7,5},{10,8},{12,10},{14,12},{11,9},... | collective-permute-start | bytes 12296 | tf_op jit(solution)/shard_map/ppermute | solution.py:21
  121.6 81.4 %collective-permute-start.12 = (f32[2,4,1,128]{3,1,2,0:T(4,128)S(1)}, f32[2,4,1,128]{3,1,2,0:T(4,128)S(1)}, u32[]{:S(2)}, u32[]{:S(2)}) collective-permute-start(f32[2,4,1,128]{3,1,2,0:T(4,128)S(1)} %get-tuple-element.260), channel_id=1, source_target_pairs={{0,2},{2,4},{4,6},{1,3},{3,5},{5,7},{8,10},{10,12},{12,14},{9,11},... | collective-permute-start | bytes 12296 | tf_op jit(solution)/shard_map/ppermute | solution.py:18
  203.2 6.4 %collective-permute-start.15 = (f32[2,4,34,1]{3,1,2,0:T(4,128)S(1)}, f32[2,4,34,1]{3,1,2,0:T(4,128)S(1)}, u32[]{:S(2)}, u32[]{:S(2)}) collective-permute-start(f32[2,4,34,1]{3,1,2,0:T(4,128)S(1)} %get-tuple-element.255), channel_id=1, source_target_pairs={{1,0},{3,2},{5,4},{7,6},{9,8},{11,10},{13,12},{15,14},{17,16},{19,... | collective-permute-start | bytes 3272 | tf_op jit(solution)/shard_map/ppermute | solution.py:21
  207.0 6.9 %collective-permute-start.14 = (f32[2,4,34,1]{3,1,2,0:T(4,128)S(1)}, f32[2,4,34,1]{3,1,2,0:T(4,128)S(1)}, u32[]{:S(2)}, u32[]{:S(2)}) collective-permute-start(f32[2,4,34,1]{3,1,2,0:T(4,128)S(1)} %get-tuple-element.254), channel_id=1, source_target_pairs={{0,1},{2,3},{4,5},{6,7},{8,9},{10,11},{12,13},{14,15},{16,17},{18,... | collective-permute-start | bytes 3272 | tf_op jit(solution)/shard_map/ppermute | solution.py:18
